TPU v7x, 32 devices: a whole 2x2x4 slice. The times are simulated.
32 devices in a mesh: grp: 2 (over core), ep: 16 (over z, y, x).
Axes of the slice: x: 2, y: 2, z: 4, core: 2. Of those that a mesh axis runs over, the one named last changes fastest.
Arguments:
- out_grad: bfloat16 [16384, 2048], P(('grp', 'ep')), may hold values from -0.5 to 0.5
- probs: float32 [16384, 8], P(('grp', 'ep')), may hold values from 0.02 to 0.5
- dest: int32 [16384, 8], P(('grp', 'ep')), may hold values from -1 to 49151, as said below
- replica_owner: int32 [2, 16], P('grp'), may hold values from 0 to 15, as said below
- gate_up: bfloat16 [98304, 1536], P(('grp', 'ep')), may hold values from -6 to 6
Outputs:
- d_down: float32 [16, 768, 2048], P('ep', None, 'grp')
Inputs may be any that keep to these rules, and one draw needn't show every extreme that they name: `dest`: copies of one token name distinct rows; a device's copies to slot buffer (j, s) fill the rows of that buffer's block for the device, which is the device's ep index times 96 onward, from its start without gaps; in every draw some device fills its block of some buffer, all 96 rows, and copies beyond a block are dropped. `replica_owner`: each entry names an expert that has its primary slot on that ep index of the group.
All inputs are finite; a program needn't handle non-finite values.
Results may differ from a plain program's by a relative error of at most 0.005.
Values may be sent and summed in bfloat16 or wider, within the bound.
A program may use at most 128 MiB of HBM per device.

v0:
```python
import jax
import jax.numpy as jnp
from jax import lax
from jax.sharding import PartitionSpec as P


def on_device(out_grad, probs, dest, replica_owner, gate_up):
    n_ep = lax.axis_size("ep")
    tokens = out_grad.shape[0]
    width = out_grad.shape[1]
    top = probs.shape[1]
    cap = gate_up.shape[0] // 2
    hidden = gate_up.shape[1] // 2
    per_src = cap // n_ep
    flat = dest.reshape(-1)
    device_of = flat // (2 * cap)
    within = flat % (2 * cap)
    slot_lookup = within // cap
    place = within % per_src
    target = device_of * 2 * per_src + slot_lookup * per_src + place
    target = jnp.where(flat >= 0, target, 2 * cap)
    copy_of = (
        jnp.full((2 * cap,), -1, jnp.int32)
        .at[target]
        .set(jnp.arange(tokens * top, dtype=jnp.int32), mode="drop")
    )
    safe = jnp.maximum(copy_of, 0)
    weight = jnp.where(copy_of >= 0, probs.reshape(-1)[safe], 0.0)
    outgoing = (weight[:, None] * out_grad[safe // top].astype(jnp.float32)).astype(jnp.bfloat16)
    outgoing = outgoing.reshape(n_ep, 2, per_src, width)
    incoming = lax.all_to_all(outgoing, "ep", split_axis=0, concat_axis=2, tiled=True)
    grads = incoming.reshape(2, cap, width)
    act = jax.nn.silu(gate_up[:, :hidden].astype(jnp.float32)) * gate_up[:, hidden:].astype(
        jnp.float32
    )
    act = act.astype(jnp.bfloat16).reshape(2, cap, hidden)
    tiles = jnp.einsum("sch,scd->shd", act, grads, preferred_element_type=jnp.float32).astype(
        jnp.bfloat16
    )
    owners = replica_owner[0]
    experts = jnp.arange(n_ep, dtype=jnp.int32)
    received = lax.all_to_all(tiles[1], "ep", split_axis=0, concat_axis=0, tiled=True)
    pieces = received.reshape(n_ep, -1)
    primary = tiles[0].astype(jnp.float32)
    select = (owners[None, :] == experts[:, None]).astype(jnp.bfloat16)
    block_sums = jnp.dot(select, pieces, preferred_element_type=jnp.float32).reshape(-1, width)
    owned = lax.all_to_all(block_sums, "ep", split_axis=0, concat_axis=0, tiled=True)
    owned = owned + primary
    result = lax.psum_scatter(owned, "grp", scatter_dimension=1, tiled=True)
    return result[None]


def solution(mesh):
    in_specs = (
        P(("grp", "ep"), None),
        P(("grp", "ep"), None),
        P(("grp", "ep"), None),
        P("grp", None),
        P(("grp", "ep"), None),
    )
    out_specs = P("ep", None, "grp")
    return jax.shard_map(
        on_device, mesh=mesh, in_specs=in_specs, out_specs=out_specs, check_vma=False
    )
```

profile of v0, /device:TPU:12, one launch (start us, length us, event | category | flops | bytes accessed | tf_op | source)
XLA Modules:
  0.0 632.4 jit_solution(17132969857570626571)
XLA Ops:
  6.5 0.9 broadcast_divide_fusion
  7.4 0.7 sign_compare_fusion
  8.3 0.2 div.41
  8.6 0.2 rem.59
  8.9 0.2 ge.17
  9.3 0.2 ne.104
  9.5 0.2 compare_select_fusion
  9.7 15.5 %scatter_custom_fusion = s32[3072]{0:T(1024)S(1)} fusion(s32[4096]{0:T(1024)S(1)} %bitcast.41, s32[4096]{0:T(1024)S(1)} %iota.7, s32[]{:T(128)} %constant.55.clone.1), kind=kCustom, calls=%fused_computation.39 | custom fusion | bytes 12292 | tf_op jit(solution)/shard_map/scatter | solution.py:25
  25.3 0.8 copy.23
  26.3 17.4 %gather_fusion = f32[3072]{0:T(1024)S(1)} fusion(f32[4096]{0:T(1024)S(1)} %reshape.175, s32[3072]{0:T(1024)S(1)} %get-tuple-element.9), kind=kCustom, calls=%fused_computation | custom fusion | bytes 36864 | tf_op jit(solution)/shard_map/gather | solution.py:28
  43.8 16.0 %gather_fusion.1 = bf16[3072,2048]{1,0:T(8,128)(2,1)} fusion(bf16[512,2048]{1,0:T(8,128)(2,1)S(1)} %copy-done, s32[3072]{0:T(1024)S(1)} %get-tuple-element.10), kind=kCustom, calls=%fused_computation.1 | custom fusion | bytes 25178112 | tf_op jit(solution)/shard_map/gather | solution.py:29
  59.8 11.1 %fusion = bf16[16,2,96,2048]{3,2,1,0:T(8,128)(2,1)} fusion(bf16[16,2,96,2048]{3,2,1,0:T(8,128)(2,1)} %bitcast.34, f32[16,2,96]{2,1,0:T(2,128)S(1)} %mul.47), kind=kLoop, calls=%fused_computation.4 | loop fusion | flops 18874368 | bytes 25178112 | tf_op jit(solution)/shard_map/convert_element_type | solution.py:29
  70.9 7.2 %all-to-all-start = ((bf16[16,2,96,2048]{3,2,1,0:T(8,128)(2,1)}), bf16[16,2,96,2048]{3,2,1,0:T(8,128)(2,1)}, u32[]{:S(2)}, u32[]{:S(2)}) async-start(bf16[16,2,96,2048]{3,2,1,0:T(8,128)(2,1)} %fusion), calls=%async_computation | async-start | bytes 25165824 | tf_op jit(solution)/shard_map/all_to_all | solution.py:31
  78.1 8.0 %fusion.5 = bf16[3072,768]{1,0:T(8,128)(2,1)} fusion(bf16[3072,1536]{1,0:T(8,128)(2,1)} %param.9), kind=kLoop, calls=%fused_computation.11 | loop fusion | flops 18874368 | bytes 14155776 | tf_op jit(solution)/shard_map/convert_element_type | solution.py:36
  86.2 276.4 %all-to-all-done = bf16[16,2,96,2048]{3,2,1,0:T(8,128)(2,1)} async-done(((bf16[16,2,96,2048]{3,2,1,0:T(8,128)(2,1)}), bf16[16,2,96,2048]{3,2,1,0:T(8,128)(2,1)}, u32[]{:S(2)}, u32[]{:S(2)}) %all-to-all-start) | async-done | bytes 12582944 | tf_op jit(solution)/shard_map/all_to_all | solution.py:31
  362.6 6.5 %copy.24 = bf16[1,2,16,96,2048]{4,3,2,1,0:T(8,128)(2,1)S(1)} copy(bf16[1,2,16,96,2048]{4,3,1,2,0:T(8,128)(2,1)} %bitcast.6) | data formatting | bytes 25165824 | tf_op jit(solution)/shard_map/all_to_all | solution.py:31
  369.1 12.0 %convolution_convert_fusion = bf16[2,768,2048]{2,1,0:T(8,128)(2,1)} fusion(bf16[2,1536,768]{2,1,0:T(8,128)(2,1)S(1)} %bitcast.40, bf16[2,1536,2048]{2,1,0:T(8,128)(2,1)S(1)} %bitcast.35), kind=kOutput, calls=%fused_computation.13 | convolution fusion | flops 9666822144 | bytes 23592960 | tf_op jit(solution)/shard_map/sch,scd->shd/dot_general | solution.py:37
  381.1 1.9 slice-done.2
  383.0 76.3 %all_to_all.33 = bf16[16,48,2048]{2,1,0:T(8,128)(2,1)S(1)} all-to-all(bf16[16,48,2048]{2,1,0:T(8,128)(2,1)S(1)} %bitcast.38), channel_id=1, replica_groups=mesh['grp'=2,'ep'=16] {'ep'}, dimensions={0} | all-to-all | bytes 6291456 | tf_op jit(solution)/shard_map/all_to_all | solution.py:42
  459.3 3.6 fusion.6
  462.9 3.6 copy.27
  466.5 141.8 %all_to_all.34 = f32[16,48,2048]{2,1,0:T(8,128)S(1)} all-to-all(f32[16,48,2048]{2,1,0:T(8,128)S(1)} %copy.27), channel_id=1, replica_groups=mesh['grp'=2,'ep'=16] {'ep'}, dimensions={0} | all-to-all | bytes 12582912 | tf_op jit(solution)/shard_map/all_to_all | solution.py:47
  608.4 3.7 convert_add_fusion
  612.1 13.5 %reduce-scatter.2.cloned.1.call-done = f32[768,1024]{1,0:T(8,128)} async-done(((f32[768,2048]{1,0:T(8,128)}), f32[768,1024]{1,0:T(8,128)}) %reduce-scatter.2.cloned.1.call-update) | async-done | bytes 3145744 | tf_op jit(solution)/shard_map/reduce_scatter | solution.py:49
  (25 shorter events, 0.9 us)
Async XLA Ops:
  6.5 37.3 %copy-start = (bf16[512,2048]{1,0:T(8,128)(2,1)S(1)}, bf16[512,2048]{1,0:T(8,128)(2,1)}, u32[]{:S(2)}) copy-start(bf16[512,2048]{1,0:T(8,128)(2,1)} %param.5) | copy-start | bytes 6291460
  70.9 291.7 %all-to-all-start = ((bf16[16,2,96,2048]{3,2,1,0:T(8,128)(2,1)}), bf16[16,2,96,2048]{3,2,1,0:T(8,128)(2,1)}, u32[]{:S(2)}, u32[]{:S(2)}) async-start(bf16[16,2,96,2048]{3,2,1,0:T(8,128)(2,1)} %fusion), calls=%async_computation | async-start | bytes 25165824 | tf_op jit(solution)/shard_map/all_to_all | solution.py:31
  78.1 547.4 %reduce-scatter.2.cloned.1.call-start = ((), (), s32[]{:S(2)}) async-start(), calls=%async_computation.4 | async-start | bytes 9437184 | tf_op jit(solution)/shard_map/reduce_scatter | solution.py:49
  362.6 6.5 %copy-start.2 = (bf16[3072,768]{1,0:T(8,128)(2,1)S(1)}, bf16[3072,768]{1,0:T(8,128)(2,1)}, u32[]{:S(2)}) copy-start(bf16[3072,768]{1,0:T(8,128)(2,1)} %fusion.5) | copy-start | bytes 14155780
  381.1 1.9 slice-start.2
  381.1 78.2 %copy-start.3 = (s32[1,16]{1,0:T(1,128)S(1)}, s32[1,16]{1,0:T(1,128)}, u32[]{:S(2)}) copy-start(s32[1,16]{1,0:T(1,128)} %param.8) | copy-start | bytes 196
  462.9 145.5 %slice-start = ((s8[6291456]{0:T(1024)(128)(4,1)}), s8[4194304]{0:T(1024)(128)(4,1)S(1)}, s32[]{:S(2)}) async-start(s8[6291456]{0:T(1024)(128)(4,1)} %bitcast.36), calls=%async_computation.5 | async-start | bytes 8388608
  466.5 141.8 %slice-start.1 = ((s8[6291456]{0:T(1024)(128)(4,1)}), s8[2097152]{0:T(1024)(128)(4,1)S(1)}, s32[]{:S(2)}) async-start(s8[6291456]{0:T(1024)(128)(4,1)} %bitcast.36), calls=%async_computation.6 | async-start | bytes 4194304
  608.4 17.2 %copy-start.1 = (bf16[512,2048]{1,0:T(8,128)(2,1)S(1)}, bf16[512,2048]{1,0:T(8,128)(2,1)}, u32[]{:S(2)}) copy-start(bf16[512,2048]{1,0:T(8,128)(2,1)} %param.5) | copy-start | bytes 6291460
Sparse Core Ops, SparseCore 0:
  612.2 13.2 reduce-scatter.1
where the time goes:
time: 634 us; the launch traced here: 632 us
  waiting for transfers between devices  290 us (46%)
  blocking collectives  218 us (34%)
  local copies, waits for them, and re-layouts  63.3 us (10%)
  other arithmetic  24.7 us (4%)
  matrix products  15.6 us (2%)
  between operations  13.6 us (2%)
  starting transfers between devices  7.2 us (1%)
    all_to_all x1, waiting for transfers between devices, on_device(): lax.all_to_all(outgoing, 'ep', split_axis=0, concat_axis=2, tiled=True)  276 us
    all_to_all x1, blocking collectives, on_device(): lax.all_to_all(block_sums, 'ep', split_axis=0, concat_axis=0, tiled=True)  142 us
    all_to_all x1, blocking collectives, on_device(): lax.all_to_all(tiles[1], 'ep', split_axis=0, concat_axis=0, tiled=True)  76.3 us
    gather x1, local copies, waits for them, and re-layouts, on_device(): weight = jnp.where(copy_of >= 0, probs.reshape(-1)[safe], 0.0)  17.4 us
    gather x1, local copies, waits for them, and re-layouts, on_device(): out_grad[safe // top].astype(jnp.float32)  16 us
    scatter x1, local copies, waits for them, and re-layouts, on_device(): copy_of = jnp.full((2 * cap,), -1, jnp.int32).at[target].set(jnp.arange(t...  15.5 us
    reduce_scatter x1, waiting for transfers between devices, on_device(): result = lax.psum_scatter(owned, 'grp', scatter_dimension=1, tiled=True)  13.5 us
  transfers between devices with their start and end apart: 2, of which 2 were waited for; matrix products, arithmetic and copies ran while one was open for 1% of the time, Pallas kernels for 0%

commit v1 on v0

v1 whole, which is shorter than its diff:
```python
import functools

import jax
import jax.numpy as jnp
from jax import lax
from jax.experimental import pallas as pl
from jax.experimental.pallas import tpu as pltpu
from jax.sharding import PartitionSpec as P

MESH = pl.DeviceIdType.MESH
LINE = 4
CHUNKS = 2
ACT_ROWS = 256


def dispatch_kernel(
    n_in, per_src, top,
    meta_hbm, og_hbm, gu_hbm, tiles_ref,
    tok, metas, sel, wgt, outb, inb, act_t, gubuf,
    ld_sem, gu_sem, zsend, zrecv, gsend, grecv, lsem,
):
    e = lax.axis_index("ep")
    z = e // n_in
    p = e % n_in
    cols = tok.shape[3]
    hidden = act_t.shape[1]
    cap = act_t.shape[2]
    block = 2 * per_src
    tokens = tok.shape[2]

    m = ((z + 1) // 2) % 2
    far, rev = (z + 2) % 4, 3 - z
    order = [z, z + 1 - 2 * (z % 2), (1 - m) * far + m * rev, (1 - m) * rev + m * far]

    def load(c):
        return pltpu.make_async_copy(
            og_hbm.at[:, pl.ds(c * cols, cols)], tok.at[c, z], ld_sem.at[c])

    def load_meta():
        return pltpu.make_async_copy(meta_hbm, metas.at[z], ld_sem.at[CHUNKS])

    def gu_load(q, slot):
        return pltpu.make_async_copy(
            gu_hbm.at[pl.ds(pl.multiple_of(q * ACT_ROWS, ACT_ROWS), ACT_ROWS), :], gubuf.at[slot], gu_sem.at[slot])

    load_meta().start()
    for c in range(CHUNKS):
        load(c).start()
    gu_load(0, 0).start()

    barrier = pltpu.get_barrier_semaphore()
    for d in range(1, n_in):
        pl.semaphore_signal(barrier, inc=1, device_id={"ep": z * n_in + (p + d) % n_in}, device_id_type=MESH)

    @pl.when(z > 0)
    def _():
        pl.semaphore_signal(barrier, inc=1, device_id={"ep": e - n_in}, device_id_type=MESH)

    @pl.when(z < LINE - 1)
    def _():
        pl.semaphore_signal(barrier, inc=1, device_id={"ep": e + n_in}, device_id_type=MESH)

    pl.semaphore_wait(barrier, n_in + m)

    def zcopy(c, zd, way):
        ref = metas.at[zd] if c == CHUNKS else tok.at[c, zd]
        return pltpu.make_async_remote_copy(
            src_ref=ref, dst_ref=ref, send_sem=zsend.at[way, c, zd], recv_sem=zrecv.at[c, zd],
            device_id={"ep": e + (n_in if way else -n_in)}, device_id_type=MESH)

    def each_hop(c, zd, act):
        parts = [CHUNKS, 0] if c == 0 else [c]

        @pl.when((zd <= z) & (z < LINE - 1))
        def _():
            for part in parts:
                act(zcopy(part, zd, 1))

        @pl.when((zd >= z) & (z > 0))
        def _():
            for part in parts:
                act(zcopy(part, zd, 0))

    def own_start(c):
        if c == 0:
            load_meta().wait()
        load(c).wait()
        each_hop(c, z, lambda copy: copy.start())

    def gcopy(c, i, d):
        zd = order[i]
        src = zd * n_in + p
        return pltpu.make_async_remote_copy(
            src_ref=outb.at[c, i, d],
            dst_ref=inb.at[c, :, pl.ds(pl.multiple_of(src * per_src, 16), per_src), :],
            send_sem=gsend.at[c, i, d], recv_sem=grecv.at[c, i, d],
            device_id={"ep": z * n_in + lax.rem(p + d, n_in)}, device_id_type=MESH)

    def lcopy(c, i):
        src = order[i] * n_in + p
        return pltpu.make_async_copy(
            outb.at[c, i, 0],
            inb.at[c, :, pl.ds(pl.multiple_of(src * per_src, 16), per_src), :], lsem.at[c, i])

    def step(c, i):
        zd = order[i]
        if i == 0:
            if c == 0:
                own_start(0)
        else:
            zcopy(c, zd, 0).wait_recv()
            if c == 0:
                zcopy(CHUNKS, zd, 0).wait_recv()
            each_hop(c, zd, lambda copy: copy.start())
        if i == 2 and c + 1 < CHUNKS:
            own_start(c + 1)

        def body(d, carry):
            pp = lax.rem(p + d, n_in)
            rows = pl.ds(pl.multiple_of(pp * block, 16), block)
            if c == 0:
                first = ((z * n_in + pp) * block).astype(jnp.float32)
                ids = lax.broadcasted_iota(jnp.int32, (block, tokens), 0).astype(jnp.float32) + first
                weights = jnp.zeros((block, tokens), jnp.float32)
                for k in range(top):
                    code = metas[zd, k:k + 1, :]
                    prob = metas[zd, top + k:top + k + 1, :]
                    weights += jnp.where(ids == code, prob, 0.0)
                sel[zd, rows, :] = jnp.where(weights != 0.0, 1.0, 0.0).astype(jnp.bfloat16)
                wgt[zd, rows, :] = jnp.broadcast_to(
                    jnp.sum(weights, axis=1, keepdims=True), (block, wgt.shape[2]))
            picked = jnp.dot(sel[zd, rows, :], tok[c, zd], preferred_element_type=jnp.float32)
            scaled = (picked * wgt[zd, rows, 0:1]).astype(jnp.bfloat16)
            outb[c, i, d] = scaled.reshape(2, per_src, cols)

            @pl.when(d > 0)
            def _():
                gcopy(c, i, d).start()

            return carry

        lax.fori_loop(0, n_in, body, 0)
        lcopy(c, i).start()

    def make_act():
        def body(q, carry):
            slot = q % 2
            gu_load(q, slot).wait()

            @pl.when(q + 1 < 2 * cap // ACT_ROWS)
            def _():
                gu_load(q + 1, 1 - slot).start()

            gate = gubuf[slot, :, :hidden].astype(jnp.float32)
            up = gubuf[slot, :, hidden:].astype(jnp.float32)
            act = (gate / (1.0 + jnp.exp(-gate)) * up).astype(jnp.bfloat16)
            s = q // (cap // ACT_ROWS)
            r = q % (cap // ACT_ROWS)
            act_t[s, :, pl.ds(pl.multiple_of(r * ACT_ROWS, ACT_ROWS), ACT_ROWS)] = act.T
            return carry

        lax.fori_loop(0, 2 * cap // ACT_ROWS, body, 0)

    def finish(c):
        for i in range(LINE):
            lcopy(c, i).wait()
            for d in range(1, n_in):
                gcopy(c, i, d).wait_recv()
        piece = 256

        def body(t, carry):
            s = t // (hidden // piece)
            r = t % (hidden // piece)
            rows = pl.ds(pl.multiple_of(r * piece, piece), piece)
            tile = jnp.dot(act_t[s, rows, :], inb[c, s], preferred_element_type=jnp.float32)
            tiles_ref[s, rows, c * cols:(c + 1) * cols] = tile.astype(jnp.bfloat16)
            return carry

        lax.fori_loop(0, 2 * (hidden // piece), body, 0)

    for c in range(CHUNKS):
        for i in range(LINE):
            step(c, i)
            if c == 0 and i == 0:
                make_act()
            if c > 0 and i == 1:
                finish(c - 1)
    finish(CHUNKS - 1)

    for c in range(CHUNKS):
        for i in range(LINE):
            each_hop(c, order[i], lambda copy: copy.wait_send())
            for d in range(1, n_in):
                gcopy(c, i, d).wait_send()


def make_tiles(meta, out_grad, gate_up, n_ep, top):
    tokens, width = out_grad.shape
    cap = gate_up.shape[0] // 2
    hidden = gate_up.shape[1] // 2
    per_src = cap // n_ep
    n_in = n_ep // LINE
    cols = width // CHUNKS
    block = 2 * per_src
    return pl.pallas_call(
        functools.partial(dispatch_kernel, n_in, per_src, top),
        out_shape=jax.ShapeDtypeStruct((2, hidden, width), jnp.bfloat16),
        in_specs=[pl.BlockSpec(memory_space=pl.ANY)] * 3,
        out_specs=pl.BlockSpec(memory_space=pltpu.VMEM),
        scratch_shapes=[
            pltpu.VMEM((CHUNKS, LINE, tokens, cols), jnp.bfloat16),
            pltpu.VMEM((LINE, 2 * top, tokens), jnp.float32),
            pltpu.VMEM((LINE, n_in * block, tokens), jnp.bfloat16),
            pltpu.VMEM((LINE, n_in * block, 128), jnp.float32),
            pltpu.VMEM((CHUNKS, LINE, n_in, 2, per_src, cols), jnp.bfloat16),
            pltpu.VMEM((CHUNKS, 2, cap, cols), jnp.bfloat16),
            pltpu.VMEM((2, hidden, cap), jnp.bfloat16),
            pltpu.VMEM((2, ACT_ROWS, 2 * hidden), jnp.bfloat16),
            pltpu.SemaphoreType.DMA((CHUNKS + 1,)),
            pltpu.SemaphoreType.DMA((2,)),
            pltpu.SemaphoreType.DMA((2, CHUNKS + 1, LINE)),
            pltpu.SemaphoreType.DMA((CHUNKS + 1, LINE)),
            pltpu.SemaphoreType.DMA((CHUNKS, LINE, n_in)),
            pltpu.SemaphoreType.DMA((CHUNKS, LINE, n_in)),
            pltpu.SemaphoreType.DMA((CHUNKS, LINE)),
        ],
        compiler_params=pltpu.CompilerParams(
            collective_id=0, has_side_effects=True, vmem_limit_bytes=66 * 1000 * 1000),
    )(meta, out_grad, gate_up)


def on_device(out_grad, probs, dest, replica_owner, gate_up):
    n_ep = lax.axis_size("ep")
    n_grp = lax.axis_size("grp")
    width = out_grad.shape[1]
    top = probs.shape[1]
    cap = gate_up.shape[0] // 2
    hidden = gate_up.shape[1] // 2
    per_src = cap // n_ep
    code = (dest // cap) * per_src + dest % per_src
    code = jnp.where(dest >= 0, code, -1)
    meta = jnp.concatenate([code.T.astype(jnp.float32), probs.T], axis=0)
    tiles = make_tiles(meta, out_grad, gate_up, n_ep, top)

    owners = lax.all_gather(replica_owner[0], "grp")
    experts = jnp.arange(n_ep, dtype=jnp.int32)
    mine = lax.all_to_all(tiles.reshape(2 * hidden, width), "grp", split_axis=1, concat_axis=0, tiled=True)
    part = width // n_grp
    mine = mine.reshape(n_grp, 2, hidden, part)
    primary = jnp.sum(mine[:, 0].astype(jnp.float32), axis=0)
    pieces = lax.all_to_all(
        mine[:, 1].reshape(n_grp, n_ep, hidden // n_ep, part), "ep", split_axis=1, concat_axis=1, tiled=True)
    pieces = pieces.reshape(n_grp * n_ep, -1)
    select = (owners.reshape(-1)[None, :] == experts[:, None]).astype(jnp.bfloat16)
    sums = jnp.dot(select, pieces, preferred_element_type=jnp.float32).astype(jnp.bfloat16)
    sums = sums.reshape(-1, part)
    owned = lax.all_to_all(sums, "ep", split_axis=0, concat_axis=0, tiled=True)
    return (owned.astype(jnp.float32) + primary)[None]


def solution(mesh):
    in_specs = (
        P(("grp", "ep"), None),
        P(("grp", "ep"), None),
        P(("grp", "ep"), None),
        P("grp", None),
        P(("grp", "ep"), None),
    )
    out_specs = P("ep", None, "grp")
    return jax.shard_map(
        on_device, mesh=mesh, in_specs=in_specs, out_specs=out_specs, check_vma=False
    )
```

time: 634 us -> 357 us (0.56)
  blocking collectives: 218 us -> 10.8 us
  waiting for transfers between devices: 290 us -> 102 us
  Pallas kernels: 0 us -> 156 us
  starting transfers between devices: 7.2 us -> 51.6 us
  local copies, waits for them, and re-layouts: 63.3 us -> 25.5 us
  other arithmetic: 24.7 us -> 9.19 us
  matrix products: 15.6 us -> 0.56 us
  between operations: 13.6 us -> 0.06 us
    all_to_all x2 -> x1, blocking collectives: 218 us -> 8.79 us  [on_device(): lax.all_to_all(tiles.reshape(2 * hidden, width), 'grp', split_axis=1, con...]
    all_to_all x1 -> x2, waiting for transfers between devices: 276 us -> 102 us  [the longest x1 68 us: on_device(): lax.all_to_all(mine[:, 1].reshape(n_grp, n_ep, hidden // n_ep, part), 'ep...]
    pallas_call x0 -> x1, Pallas kernels: none -> 156 us  [make_tiles(): pl.pallas_call(functools.partial(dispatch_kernel, n_in, per_src, top), ou...]
    all_to_all x1 -> x2, starting transfers between devices: 7.17 us -> 51.6 us  [the longest x1 46.1 us: on_device(): lax.all_to_all(mine[:, 1].reshape(n_grp, n_ep, hidden // n_ep, part), 'ep...]
    gather x2 -> x0, local copies, waits for them, and re-layouts: 33.4 us -> none  [the longest x1 17.4 us: on_device(): weight = jnp.where(copy_of >= 0, probs.reshape(-1)[safe], 0.0)]
    convert_element_type x2 -> x1, other arithmetic: 19.2 us -> 0.74 us  [on_device(): meta = jnp.concatenate([code.T.astype(jnp.float32), probs.T], axis=0)]
    scatter x1 -> x0, local copies, waits for them, and re-layouts: 15.5 us -> none  [on_device(): copy_of = jnp.full((2 * cap,), -1, jnp.int32).at[target].set(jnp.arange(t...]
    reduce_scatter x1 -> x0, waiting for transfers between devices: 13.5 us -> none  [on_device(): result = lax.psum_scatter(owned, 'grp', scatter_dimension=1, tiled=True)]
where the time goes in v1:
time: 357 us; the launch traced here: 356 us
  Pallas kernels  156 us (44%)
  waiting for transfers between devices  102 us (29%)
  starting transfers between devices  51.6 us (14%)
  local copies, waits for them, and re-layouts  25.5 us (7%)
  blocking collectives  10.8 us (3%)
  other arithmetic  9.19 us (3%)
    pallas_call x1, Pallas kernels, make_tiles(): pl.pallas_call(functools.partial(dispatch_kernel, n_in, per_src, top), ou...  156 us
    all_to_all x1, waiting for transfers between devices, on_device(): lax.all_to_all(mine[:, 1].reshape(n_grp, n_ep, hidden // n_ep, part), 'ep...  68 us
    all_to_all x1, starting transfers between devices, on_device(): lax.all_to_all(mine[:, 1].reshape(n_grp, n_ep, hidden // n_ep, part), 'ep...  46.1 us
    all_to_all x1, waiting for transfers between devices, on_device(): owned = lax.all_to_all(sums, 'ep', split_axis=0, concat_axis=0, tiled=True)  33.9 us
    all_to_all x2, local copies, waits for them, and re-layouts, on_device(): lax.all_to_all(tiles.reshape(2 * hidden, width), 'grp', split_axis=1, con...  15.9 us
    all_to_all x1, blocking collectives, on_device(): lax.all_to_all(tiles.reshape(2 * hidden, width), 'grp', split_axis=1, con...  8.79 us
  transfers between devices with their start and end apart: 2, of which 2 were waited for; matrix products, arithmetic and copies ran while one was open for 1% of the time, Pallas kernels for 0%

profile of v1, /device:TPU:12, one launch (start us, length us, event | category | flops | bytes accessed | tf_op | source)
XLA Modules:
  0.0 355.9 jit_solution(14570453432108322008)
XLA Ops:
  0.0 0.7 fusion.4
  0.7 1.3 pad_maximum_fusion.meta_hbm
  2.1 156.2 %shard_map.55 = bf16[2,768,2048]{2,1,0:T(8,128)(2,1)} custom-call(f32[16,512]{1,0:T(8,128)} %pad_maximum_fusion.meta_hbm, bf16[512,2048]{1,0:T(8,128)(2,1)} %og_hbm.1, bf16[3072,1536]{1,0:T(8,128)(2,1)} %gu_hbm.1), custom_call_target="tpu_custom_call" | custom-call | tf_op jit(solution)/shard_map/pallas_call | solution.py:205
  158.3 11.1 %all_to_all.21 = bf16[1536,2,1024]{2,1,0:T(2,128)(2,1)} reshape(bf16[2,768,2048]{2,1,0:T(8,128)(2,1)} %shard_map.55) | data formatting | bytes 12582912 | tf_op jit(solution)/shard_map/all_to_all | solution.py:247
  169.5 4.8 %copy.12 = bf16[1536,2,1024]{2,0,1:T(8,128)(2,1)S(1)} copy(bf16[1536,2,1024]{2,1,0:T(2,128)(2,1)} %all_to_all.21) | data formatting | bytes 12582912 | tf_op jit(solution)/shard_map/all_to_all | solution.py:247
  174.2 8.8 %all_to_all.30 = bf16[1536,2,1024]{2,0,1:T(8,128)(2,1)S(1)} all-to-all(bf16[1536,2,1024]{2,0,1:T(8,128)(2,1)S(1)} %copy.12), channel_id=1, replica_groups=mesh['grp'=2,'ep'=16] {'grp'}, dimensions={1} | all-to-all | bytes 12582912 | tf_op jit(solution)/shard_map/all_to_all | solution.py:247
  183.0 0.3 slice.8
  183.3 2.3 copy-done
  185.7 2.2 copy.13
  187.8 46.1 %all-to-all-start.1 = ((bf16[2,16,48,1024]{3,2,0,1:T(8,128)(2,1)}), bf16[2,16,48,1024]{3,2,0,1:T(8,128)(2,1)S(1)}, u32[]{:S(2)}, u32[]{:S(2)}) async-start(bf16[2,16,48,1024]{3,2,0,1:T(8,128)(2,1)} %copy.13), calls=%async_computation.1 | async-start | bytes 6291456 | tf_op jit(solution)/shard_map/all_to_all | solution.py:251
  233.9 0.0 copy-done.1
  233.9 2.0 all-gather
  235.9 0.5 broadcast.6
  236.5 0.7 reduce.4
  237.1 0.1 eq.17
  237.2 68.0 %all-to-all-done.1 = bf16[2,16,48,1024]{3,2,0,1:T(8,128)(2,1)S(1)} async-done(((bf16[2,16,48,1024]{3,2,0,1:T(8,128)(2,1)}), bf16[2,16,48,1024]{3,2,0,1:T(8,128)(2,1)S(1)}, u32[]{:S(2)}, u32[]{:S(2)}) %all-to-all-start.1) | async-done | bytes 3145760 | tf_op jit(solution)/shard_map/all_to_all | solution.py:251
  305.2 0.4 copy.14
  305.6 1.7 copy.15
  307.4 0.6 convolution_convert_fusion
  307.9 2.0 copy.16
  309.9 5.5 %all-to-all-start.2 = ((bf16[16,48,1024]{2,1,0:T(8,128)(2,1)}), bf16[16,48,1024]{2,1,0:T(8,128)(2,1)}, u32[]{:S(2)}, u32[]{:S(2)}) async-start(bf16[16,48,1024]{2,1,0:T(8,128)(2,1)} %bitcast.14), calls=%async_computation.2 | async-start | bytes 3145728 | tf_op jit(solution)/shard_map/all_to_all | solution.py:257
  315.5 2.9 convert_reduce_fusion
  318.4 33.9 %all-to-all-done.2 = bf16[16,48,1024]{2,1,0:T(8,128)(2,1)} async-done(((bf16[16,48,1024]{2,1,0:T(8,128)(2,1)}), bf16[16,48,1024]{2,1,0:T(8,128)(2,1)}, u32[]{:S(2)}, u32[]{:S(2)}) %all-to-all-start.2) | async-done | bytes 1572896 | tf_op jit(solution)/shard_map/all_to_all | solution.py:257
  352.3 3.5 convert_add_fusion
  (2 shorter events, 0.0 us)
Async XLA Ops:
  183.0 2.7 copy-start
  187.8 46.1 %copy-start.1 = (s32[1,16]{1,0:T(1,128)S(1)}, s32[1,16]{1,0:T(1,128)}, u32[]{:S(2)}) copy-start(s32[1,16]{1,0:T(1,128)} %param.8) | copy-start | bytes 196
  187.8 117.4 %all-to-all-start.1 = ((bf16[2,16,48,1024]{3,2,0,1:T(8,128)(2,1)}), bf16[2,16,48,1024]{3,2,0,1:T(8,128)(2,1)S(1)}, u32[]{:S(2)}, u32[]{:S(2)}) async-start(bf16[2,16,48,1024]{3,2,0,1:T(8,128)(2,1)} %copy.13), calls=%async_computation.1 | async-start | bytes 6291456 | tf_op jit(solution)/shard_map/all_to_all | solution.py:251
  309.9 42.4 %all-to-all-start.2 = ((bf16[16,48,1024]{2,1,0:T(8,128)(2,1)}), bf16[16,48,1024]{2,1,0:T(8,128)(2,1)}, u32[]{:S(2)}, u32[]{:S(2)}) async-start(bf16[16,48,1024]{2,1,0:T(8,128)(2,1)} %bitcast.14), calls=%async_computation.2 | async-start | bytes 3145728 | tf_op jit(solution)/shard_map/all_to_all | solution.py:257

commit v2 on v1

v2 whole, which is shorter than its diff:
```python
import functools

import jax
import jax.numpy as jnp
from jax import lax
from jax.experimental import pallas as pl
from jax.experimental.pallas import tpu as pltpu
from jax.sharding import PartitionSpec as P

MESH = pl.DeviceIdType.MESH
LINE = 4
CHUNKS = 2
ACT_ROWS = 128


def dispatch_kernel(
    n_ep, n_grp, per_src, top,
    owners, meta_hbm, og_hbm, gu_hbm, out_ref,
    tok, metas, sel, wgt, outb, inb, act_t, gubuf,
    tiles, mine, pieces, sums, back,
    ld_sem, gu_sem, zsend, zrecv, gsend, grecv,
    asend, arecv, bsend, brecv, dsend, drecv,
):
    n_in = n_ep // LINE
    g = lax.axis_index("grp")
    e = lax.axis_index("ep")
    share = mine.shape[5]
    share_cols = pl.ds(pl.multiple_of(g * share, 128), share)
    z = e // n_in
    p = e % n_in
    cols = tok.shape[3]
    hidden = act_t.shape[1]
    cap = act_t.shape[2]
    block = 2 * per_src
    tokens = tok.shape[2]

    m = ((z + 1) // 2) % 2
    far, rev = (z + 2) % 4, 3 - z
    order = [z, z + 1 - 2 * (z % 2), (1 - m) * far + m * rev, (1 - m) * rev + m * far]

    def load(c, part):
        return pltpu.make_async_copy(
            og_hbm.at[:, pl.ds((part * CHUNKS + c) * share, share)],
            tok.at[c, z, :, pl.ds(part * share, share)], ld_sem.at[c, part])

    def load_meta():
        return pltpu.make_async_copy(meta_hbm, metas.at[z], ld_sem.at[CHUNKS, 0])

    def gu_load(q, slot):
        return pltpu.make_async_copy(
            gu_hbm.at[pl.ds(pl.multiple_of(q * ACT_ROWS, ACT_ROWS), ACT_ROWS), :], gubuf.at[slot], gu_sem.at[slot])

    load_meta().start()
    for c in range(CHUNKS):
        for part in range(n_grp):
            load(c, part).start()
    gu_load(0, 0).start()

    barrier = pltpu.get_barrier_semaphore()
    def greet(d, carry):
        pl.semaphore_signal(barrier, inc=1, device_id={"ep": lax.rem(e + d, n_ep)}, device_id_type=MESH)
        return carry

    lax.fori_loop(1, n_ep, greet, 0)
    for d in range(1, n_grp):
        pl.semaphore_signal(barrier, inc=1, device_id={"grp": lax.rem(g + d, n_grp)}, device_id_type=MESH)
    pl.semaphore_wait(barrier, n_ep + n_grp - 2)

    def zcopy(c, zd, way):
        ref = metas.at[zd] if c == CHUNKS else tok.at[c, zd]
        return pltpu.make_async_remote_copy(
            src_ref=ref, dst_ref=ref, send_sem=zsend.at[way, c, zd], recv_sem=zrecv.at[c, zd],
            device_id={"ep": e + (n_in if way else -n_in)}, device_id_type=MESH)

    def each_hop(c, zd, act):
        parts = [CHUNKS, 0] if c == 0 else [c]

        @pl.when((zd <= z) & (z < LINE - 1))
        def _():
            for part in parts:
                act(zcopy(part, zd, 1))

        @pl.when((zd >= z) & (z > 0))
        def _():
            for part in parts:
                act(zcopy(part, zd, 0))

    def own_start(c):
        if c == 0:
            load_meta().wait()
        for part in range(n_grp):
            load(c, part).wait()
        each_hop(c, z, lambda copy: copy.start())

    def gcopy(c, i, d):
        zd = order[i]
        src = zd * n_in + p
        return pltpu.make_async_remote_copy(
            src_ref=outb.at[c, i, d - 1],
            dst_ref=inb.at[c, :, pl.ds(pl.multiple_of(src * per_src, 16), per_src), :],
            send_sem=gsend.at[c, i, d - 1], recv_sem=grecv.at[c, i, d - 1],
            device_id={"ep": z * n_in + lax.rem(p + d, n_in)}, device_id_type=MESH)

    def step(c, i):
        zd = order[i]
        if i == 0:
            if c == 0:
                own_start(0)
        else:
            zcopy(c, zd, 0).wait_recv()
            if c == 0:
                zcopy(CHUNKS, zd, 0).wait_recv()
            each_hop(c, zd, lambda copy: copy.start())
        if i == 2 and c + 1 < CHUNKS:
            own_start(c + 1)

        def body(d, carry):
            pp = lax.rem(p + d, n_in)
            rows = pl.ds(pl.multiple_of(pp * block, 16), block)
            if c == 0:
                first = ((z * n_in + pp) * block).astype(jnp.float32)
                ids = lax.broadcasted_iota(jnp.int32, (block, tokens), 0).astype(jnp.float32) + first
                weights = jnp.zeros((block, tokens), jnp.float32)
                for k in range(top):
                    code = metas[zd, k:k + 1, :]
                    prob = metas[zd, top + k:top + k + 1, :]
                    weights += jnp.where(ids == code, prob, 0.0)
                sel[zd, rows, :] = jnp.where(weights != 0.0, 1.0, 0.0).astype(jnp.bfloat16)
                wgt[zd, rows, :] = jnp.broadcast_to(
                    jnp.sum(weights, axis=1, keepdims=True), (block, wgt.shape[2]))
            picked = jnp.dot(sel[zd, rows, :], tok[c, zd], preferred_element_type=jnp.float32)
            scaled = (picked * wgt[zd, rows, 0:1]).astype(jnp.bfloat16)
            scaled = scaled.reshape(2, per_src, cols)

            @pl.when(d == 0)
            def _():
                own = pl.ds(pl.multiple_of((zd * n_in + p) * per_src, 16), per_src)
                inb[c, :, own, :] = scaled

            @pl.when(d > 0)
            def _():
                outb[c, i, d - 1] = scaled
                gcopy(c, i, d).start()

            return carry

        lax.fori_loop(0, n_in, body, 0)

    def make_act():
        def body(q, carry):
            slot = q % 2
            gu_load(q, slot).wait()

            @pl.when(q + 1 < 2 * cap // ACT_ROWS)
            def _():
                gu_load(q + 1, 1 - slot).start()

            gate = gubuf[slot, :, :hidden].astype(jnp.float32)
            up = gubuf[slot, :, hidden:].astype(jnp.float32)
            act = (gate / (1.0 + jnp.exp(-gate)) * up).astype(jnp.bfloat16)
            s = q // (cap // ACT_ROWS)
            r = q % (cap // ACT_ROWS)
            act_t[s, :, pl.ds(pl.multiple_of(r * ACT_ROWS, ACT_ROWS), ACT_ROWS)] = act.T
            return carry

        lax.fori_loop(0, 2 * cap // ACT_ROWS, body, 0)

    def multiply(c, s):
        group = n_ep // LINE

        def body(r, carry):
            rows = pl.ds(pl.multiple_of(r * (hidden // LINE), 16), hidden // LINE)
            tile = jnp.dot(act_t[s, rows, :], inb[c, s], preferred_element_type=jnp.float32)
            tiles[c, s, pl.ds(r * group, group)] = tile.reshape(
                group, hidden // n_ep, cols).astype(jnp.bfloat16)
            return carry

        lax.fori_loop(0, LINE, body, 0)

    def swap(c, s, d):
        there = lax.rem(g + d, n_grp)
        return pltpu.make_async_remote_copy(
            src_ref=tiles.at[c, s, :, :, pl.ds(pl.multiple_of(there * share, 128), share)],
            dst_ref=mine.at[c, d - 1, s],
            send_sem=asend.at[c, s, d - 1], recv_sem=arecv.at[c, s, d - 1],
            device_id={"grp": there}, device_id_type=MESH)

    def spread(c, gd, d):
        there = lax.rem(e + d, n_ep)
        src = tiles.at[c, 1, there, :, share_cols] if gd == 0 else mine.at[c, gd - 1, 1, there]
        return pltpu.make_async_remote_copy(
            src_ref=src, dst_ref=pieces.at[c, gd, e],
            send_sem=bsend.at[c, gd, d], recv_sem=brecv.at[c, gd, d],
            device_id={"ep": there}, device_id_type=MESH)

    def spread_own(c, gd):
        src = tiles.at[c, 1, e, :, share_cols] if gd == 0 else mine.at[c, gd - 1, 1, e]
        return pltpu.make_async_copy(src, pieces.at[c, gd, e], bsend.at[c, gd, 0])

    def give(c, d):
        there = lax.rem(e + d, n_ep)
        return pltpu.make_async_remote_copy(
            src_ref=sums.at[c, there], dst_ref=back.at[c, e],
            send_sem=dsend.at[c, d], recv_sem=drecv.at[c, d],
            device_id={"ep": there}, device_id_type=MESH)

    def give_own(c):
        return pltpu.make_async_copy(sums.at[c, e], back.at[c, e], dsend.at[c, 0])

    def peers(act):
        def body(d, carry):
            act(d)
            return carry

        lax.fori_loop(1, n_ep, body, 0)

    def tail_a(c):
        for i in range(LINE):
            for d in range(1, n_in):
                gcopy(c, i, d).wait_recv()
        multiply(c, 1)
        for d in range(1, n_grp):
            swap(c, 1, d).start()
        peers(lambda d: spread(c, 0, d).start())
        spread_own(c, 0).start()
        multiply(c, 0)
        for d in range(1, n_grp):
            swap(c, 0, d).start()

    def tail_b(c):
        for gd in range(1, n_grp):
            swap(c, 1, gd).wait_recv()
            peers(lambda d: spread(c, gd, d).start())
            spread_own(c, gd).start()

    def tail_c(c):
        for gd in range(n_grp):
            spread_own(c, gd).wait()
            peers(lambda d: spread(c, gd, d).wait_recv())
        batch = 4
        height = hidden // n_ep

        def body(t, carry):
            lane = pl.ds(pl.multiple_of((t // (n_ep // batch)) * 128, 128), 128)
            first = (t % (n_ep // batch)) * batch

            def add(j, totals):
                for gd in range(n_grp):
                    owner = owners[lax.rem(g + n_grp - gd, n_grp), j]
                    piece = pieces[c, gd, j, :, lane].astype(jnp.float32)
                    totals = tuple(
                        total + piece * jnp.where(owner == first + b, 1.0, 0.0)
                        for b, total in enumerate(totals))
                return totals

            totals = lax.fori_loop(
                0, n_ep, add, tuple(jnp.zeros((height, 128), jnp.float32) for _ in range(batch)))
            for b in range(batch):
                sums[c, first + b, :, lane] = totals[b].astype(jnp.bfloat16)
            return carry

        lax.fori_loop(0, (share // 128) * (n_ep // batch), body, 0)
        peers(lambda d: give(c, d).start())
        give_own(c).start()

    def tail_d(c):
        for d in range(1, n_grp):
            swap(c, 0, d).wait_recv()
        give_own(c).wait()
        peers(lambda d: give(c, d).wait_recv())

        def body(r, carry):
            total = tiles[c, 0, r, :, share_cols].astype(jnp.float32)
            for gd in range(1, n_grp):
                total += mine[c, gd - 1, 0, r].astype(jnp.float32)
            out_ref[r, :, c * share:(c + 1) * share] = total + back[c, r].astype(jnp.float32)
            return carry

        lax.fori_loop(0, n_ep, body, 0)

    for c in range(CHUNKS):
        for i in range(LINE):
            step(c, i)
            if c == 0 and i == 0:
                make_act()
            if c > 0 and i == 0:
                tail_a(c - 1)
            if c > 0 and i == 1:
                tail_b(c - 1)
            if c > 0 and i == LINE - 1:
                tail_c(c - 1)
    tail_a(CHUNKS - 1)
    tail_b(CHUNKS - 1)
    for c in range(CHUNKS - 1):
        tail_d(c)
    tail_c(CHUNKS - 1)
    tail_d(CHUNKS - 1)

    for c in range(CHUNKS):
        for i in range(LINE):
            each_hop(c, order[i], lambda copy: copy.wait_send())
            for d in range(1, n_in):
                gcopy(c, i, d).wait_send()
        for d in range(1, n_grp):
            swap(c, 0, d).wait_send()
            swap(c, 1, d).wait_send()
        for gd in range(n_grp):
            peers(lambda d: spread(c, gd, d).wait_send())
        peers(lambda d: give(c, d).wait_send())


def run_kernel(owners, meta, out_grad, gate_up, n_ep, n_grp, top):
    tokens, width = out_grad.shape
    cap = gate_up.shape[0] // 2
    hidden = gate_up.shape[1] // 2
    per_src = cap // n_ep
    n_in = n_ep // LINE
    cols = width // CHUNKS
    share = cols // n_grp
    height = hidden // n_ep
    block = 2 * per_src
    bf16 = jnp.bfloat16
    dma = pltpu.SemaphoreType.DMA
    return pl.pallas_call(
        functools.partial(dispatch_kernel, n_ep, n_grp, per_src, top),
        out_shape=jax.ShapeDtypeStruct((n_ep, height, width // n_grp), jnp.float32),
        in_specs=[pl.BlockSpec(memory_space=pltpu.SMEM)] + [pl.BlockSpec(memory_space=pl.ANY)] * 3,
        out_specs=pl.BlockSpec(memory_space=pltpu.VMEM),
        scratch_shapes=[
            pltpu.VMEM((CHUNKS, LINE, tokens, cols), bf16),
            pltpu.VMEM((LINE, 2 * top, tokens), jnp.float32),
            pltpu.VMEM((LINE, n_in * block, tokens), bf16),
            pltpu.VMEM((LINE, n_in * block, 128), jnp.float32),
            pltpu.VMEM((CHUNKS, LINE, n_in - 1, 2, per_src, cols), bf16),
            pltpu.VMEM((CHUNKS, 2, cap, cols), bf16),
            pltpu.VMEM((2, hidden, cap), bf16),
            pltpu.VMEM((2, ACT_ROWS, 2 * hidden), bf16),
            pltpu.VMEM((CHUNKS, 2, n_ep, height, cols), bf16),
            pltpu.VMEM((CHUNKS, n_grp - 1, 2, n_ep, height, share), bf16),
            pltpu.VMEM((CHUNKS, n_grp, n_ep, height, share), bf16),
            pltpu.VMEM((CHUNKS, n_ep, height, share), bf16),
            pltpu.VMEM((CHUNKS, n_ep, height, share), bf16),
            dma((CHUNKS + 1, n_grp)),
            dma((2,)),
            dma((2, CHUNKS + 1, LINE)),
            dma((CHUNKS + 1, LINE)),
            dma((CHUNKS, LINE, n_in - 1)),
            dma((CHUNKS, LINE, n_in - 1)),
            dma((CHUNKS, 2, n_grp - 1)),
            dma((CHUNKS, 2, n_grp - 1)),
            dma((CHUNKS, n_grp, n_ep)),
            dma((CHUNKS, n_grp, n_ep)),
            dma((CHUNKS, n_ep)),
            dma((CHUNKS, n_ep)),
        ],
        compiler_params=pltpu.CompilerParams(
            collective_id=0, has_side_effects=True, vmem_limit_bytes=67043328),
    )(owners, meta, out_grad, gate_up)


def on_device(out_grad, probs, dest, replica_owner, gate_up):
    n_ep = lax.axis_size("ep")
    n_grp = lax.axis_size("grp")
    top = probs.shape[1]
    cap = gate_up.shape[0] // 2
    hidden = gate_up.shape[1] // 2
    per_src = cap // n_ep
    code = (dest // cap) * per_src + dest % per_src
    code = jnp.where(dest >= 0, code, -1)
    meta = jnp.concatenate([code.T.astype(jnp.float32), probs.T], axis=0)
    owners = lax.all_gather(replica_owner[0], "grp")
    total = run_kernel(owners, meta, out_grad, gate_up, n_ep, n_grp, top)
    return total.reshape(1, hidden, -1)


def solution(mesh):
    in_specs = (
        P(("grp", "ep"), None),
        P(("grp", "ep"), None),
        P(("grp", "ep"), None),
        P("grp", None),
        P(("grp", "ep"), None),
    )
    out_specs = P("ep", None, "grp")
    return jax.shard_map(
        on_device, mesh=mesh, in_specs=in_specs, out_specs=out_specs, check_vma=False
    )
```

time: 357 us -> 296 us (0.83)
  Pallas kernels: 156 us -> 286 us
  waiting for transfers between devices: 102 us -> 0 us
  starting transfers between devices: 51.6 us -> 0 us
  local copies, waits for them, and re-layouts: 25.5 us -> 3.97 us
  blocking collectives: 10.8 us -> 2.93 us
  other arithmetic: 9.19 us -> 2.08 us
    pallas_call x1, Pallas kernels: 156 us -> 286 us  [run_kernel(): pl.pallas_call(functools.partial(dispatch_kernel, n_ep, n_grp, per_src, t...]
    all_to_all x2 -> x0, waiting for transfers between devices: 102 us -> none  [the longest x1 68 us: on_device(): lax.all_to_all(mine[:, 1].reshape(n_grp, n_ep, hidden // n_ep, part), 'ep...]
    all_to_all x2 -> x0, starting transfers between devices: 51.6 us -> none  [the longest x1 46.1 us: on_device(): lax.all_to_all(mine[:, 1].reshape(n_grp, n_ep, hidden // n_ep, part), 'ep...]
    all_to_all x3 -> x0, local copies, waits for them, and re-layouts: 16.3 us -> none  [the longest x2 15.9 us: on_device(): lax.all_to_all(tiles.reshape(2 * hidden, width), 'grp', split_axis=1, con...]
    all_to_all x1 -> x0, blocking collectives: 8.79 us -> none  [on_device(): lax.all_to_all(tiles.reshape(2 * hidden, width), 'grp', split_axis=1, con...]
  transfers between devices with their start and end apart: 2 -> 0, of which waited for: 2 -> 0; matrix products, arithmetic and copies ran while one was open for 1% -> 0% of each run, Pallas kernels for 0% -> 0%
where the time goes in v2:
time: 296 us; the launch traced here: 295 us
  Pallas kernels  286 us (97%)
  local copies, waits for them, and re-layouts  3.97 us (1%)
    pallas_call x1, Pallas kernels, run_kernel(): pl.pallas_call(functools.partial(dispatch_kernel, n_ep, n_grp, per_src, t...  286 us

profile of v2, /device:TPU:12, one launch (start us, length us, event | category | flops | bytes accessed | tf_op | source)
XLA Modules:
  0.0 295.0 jit_solution(9815010759347647994)
XLA Ops:
  0.0 2.9 all-gather
  2.9 0.7 fusion.4
  3.7 1.3 pad_maximum_fusion.meta_hbm
  5.0 286.0 %shard_map.55 = f32[16,48,1024]{2,1,0:T(8,128)} custom-call(s32[2,16]{1,0:T(2,128)} %bitcast.8, f32[16,512]{1,0:T(8,128)} %pad_maximum_fusion.meta_hbm, bf16[512,2048]{1,0:T(8,128)(2,1)} %og_hbm.1, bf16[3072,1536]{1,0:T(8,128)(2,1)} %gu_hbm.1), custom_call_target="tpu_custom_call" | custom-call | tf_op jit(solution)/shard_map/pallas_call | solution.py:324
  291.1 4.0 %copy.7 = f32[1,768,1024]{2,1,0:T(8,128)} copy(f32[1,768,1024]{2,1,0:T(8,128)} %bitcast.6) | data formatting | bytes 6291456

commit v3 on v2

--- a/solution.py
+++ b/solution.py
@@ -9,12 +9,13 @@
 
 MESH = pl.DeviceIdType.MESH
 LINE = 4
-CHUNKS = 2
+MAX_CHUNKS = 4
+NEXT_AT = 1
 ACT_ROWS = 128
 
 
 def dispatch_kernel(
-    n_ep, n_grp, per_src, top,
+    n_ep, n_grp, per_src, top, chunks,
     owners, meta_hbm, og_hbm, gu_hbm, out_ref,
     tok, metas, sel, wgt, outb, inb, act_t, gubuf,
     tiles, mine, pieces, sums, back,
@@ -40,18 +41,18 @@
 
     def load(c, part):
         return pltpu.make_async_copy(
-            og_hbm.at[:, pl.ds((part * CHUNKS + c) * share, share)],
+            og_hbm.at[:, pl.ds((part * chunks + c) * share, share)],
             tok.at[c, z, :, pl.ds(part * share, share)], ld_sem.at[c, part])
 
     def load_meta():
-        return pltpu.make_async_copy(meta_hbm, metas.at[z], ld_sem.at[CHUNKS, 0])
+        return pltpu.make_async_copy(meta_hbm, metas.at[z], ld_sem.at[chunks, 0])
 
     def gu_load(q, slot):
         return pltpu.make_async_copy(
             gu_hbm.at[pl.ds(pl.multiple_of(q * ACT_ROWS, ACT_ROWS), ACT_ROWS), :], gubuf.at[slot], gu_sem.at[slot])
 
     load_meta().start()
-    for c in range(CHUNKS):
+    for c in range(chunks):
         for part in range(n_grp):
             load(c, part).start()
     gu_load(0, 0).start()
@@ -67,13 +68,13 @@
     pl.semaphore_wait(barrier, n_ep + n_grp - 2)
 
     def zcopy(c, zd, way):
-        ref = metas.at[zd] if c == CHUNKS else tok.at[c, zd]
+        ref = metas.at[zd] if c == chunks else tok.at[c, zd]
         return pltpu.make_async_remote_copy(
             src_ref=ref, dst_ref=ref, send_sem=zsend.at[way, c, zd], recv_sem=zrecv.at[c, zd],
             device_id={"ep": e + (n_in if way else -n_in)}, device_id_type=MESH)
 
     def each_hop(c, zd, act):
-        parts = [CHUNKS, 0] if c == 0 else [c]
+        parts = [chunks, 0] if c == 0 else [c]
 
         @pl.when((zd <= z) & (z < LINE - 1))
         def _():
@@ -109,9 +110,9 @@
         else:
             zcopy(c, zd, 0).wait_recv()
             if c == 0:
-                zcopy(CHUNKS, zd, 0).wait_recv()
+                zcopy(chunks, zd, 0).wait_recv()
             each_hop(c, zd, lambda copy: copy.start())
-        if i == 2 and c + 1 < CHUNKS:
+        if i == NEXT_AT and c + 1 < chunks:
             own_start(c + 1)
 
         def body(d, carry):
@@ -278,7 +279,7 @@
 
         lax.fori_loop(0, n_ep, body, 0)
 
-    for c in range(CHUNKS):
+    for c in range(chunks):
         for i in range(LINE):
             step(c, i)
             if c == 0 and i == 0:
@@ -287,16 +288,18 @@
                 tail_a(c - 1)
             if c > 0 and i == 1:
                 tail_b(c - 1)
-            if c > 0 and i == LINE - 1:
-                tail_c(c - 1)
-    tail_a(CHUNKS - 1)
-    tail_b(CHUNKS - 1)
-    for c in range(CHUNKS - 1):
+            if c > 1 and i == 1:
+                tail_c(c - 2)
+    tail_a(chunks - 1)
+    tail_b(chunks - 1)
+    if chunks > 1:
+        tail_c(chunks - 2)
+    for c in range(chunks - 1):
         tail_d(c)
-    tail_c(CHUNKS - 1)
-    tail_d(CHUNKS - 1)
-
-    for c in range(CHUNKS):
+    tail_c(chunks - 1)
+    tail_d(chunks - 1)
+
+    for c in range(chunks):
         for i in range(LINE):
             each_hop(c, order[i], lambda copy: copy.wait_send())
             for d in range(1, n_in):
@@ -315,43 +318,44 @@
     hidden = gate_up.shape[1] // 2
     per_src = cap // n_ep
     n_in = n_ep // LINE
-    cols = width // CHUNKS
+    chunks = max(1, min(MAX_CHUNKS, width // n_grp // 128))
+    cols = width // chunks
     share = cols // n_grp
     height = hidden // n_ep
     block = 2 * per_src
     bf16 = jnp.bfloat16
     dma = pltpu.SemaphoreType.DMA
     return pl.pallas_call(
-        functools.partial(dispatch_kernel, n_ep, n_grp, per_src, top),
+        functools.partial(dispatch_kernel, n_ep, n_grp, per_src, top, chunks),
         out_shape=jax.ShapeDtypeStruct((n_ep, height, width // n_grp), jnp.float32),
         in_specs=[pl.BlockSpec(memory_space=pltpu.SMEM)] + [pl.BlockSpec(memory_space=pl.ANY)] * 3,
         out_specs=pl.BlockSpec(memory_space=pltpu.VMEM),
         scratch_shapes=[
-            pltpu.VMEM((CHUNKS, LINE, tokens, cols), bf16),
+            pltpu.VMEM((chunks, LINE, tokens, cols), bf16),
             pltpu.VMEM((LINE, 2 * top, tokens), jnp.float32),
             pltpu.VMEM((LINE, n_in * block, tokens), bf16),
             pltpu.VMEM((LINE, n_in * block, 128), jnp.float32),
-            pltpu.VMEM((CHUNKS, LINE, n_in - 1, 2, per_src, cols), bf16),
-            pltpu.VMEM((CHUNKS, 2, cap, cols), bf16),
+            pltpu.VMEM((chunks, LINE, n_in - 1, 2, per_src, cols), bf16),
+            pltpu.VMEM((chunks, 2, cap, cols), bf16),
             pltpu.VMEM((2, hidden, cap), bf16),
             pltpu.VMEM((2, ACT_ROWS, 2 * hidden), bf16),
-            pltpu.VMEM((CHUNKS, 2, n_ep, height, cols), bf16),
-            pltpu.VMEM((CHUNKS, n_grp - 1, 2, n_ep, height, share), bf16),
-            pltpu.VMEM((CHUNKS, n_grp, n_ep, height, share), bf16),
-            pltpu.VMEM((CHUNKS, n_ep, height, share), bf16),
-            pltpu.VMEM((CHUNKS, n_ep, height, share), bf16),
-            dma((CHUNKS + 1, n_grp)),
+            pltpu.VMEM((chunks, 2, n_ep, height, cols), bf16),
+            pltpu.VMEM((chunks, n_grp - 1, 2, n_ep, height, share), bf16),
+            pltpu.VMEM((chunks, n_grp, n_ep, height, share), bf16),
+            pltpu.VMEM((chunks, n_ep, height, share), bf16),
+            pltpu.VMEM((chunks, n_ep, height, share), bf16),
+            dma((chunks + 1, n_grp)),
             dma((2,)),
-            dma((2, CHUNKS + 1, LINE)),
-            dma((CHUNKS + 1, LINE)),
-            dma((CHUNKS, LINE, n_in - 1)),
-            dma((CHUNKS, LINE, n_in - 1)),
-            dma((CHUNKS, 2, n_grp - 1)),
-            dma((CHUNKS, 2, n_grp - 1)),
-            dma((CHUNKS, n_grp, n_ep)),
-            dma((CHUNKS, n_grp, n_ep)),
-            dma((CHUNKS, n_ep)),
-            dma((CHUNKS, n_ep)),
+            dma((2, chunks + 1, LINE)),
+            dma((chunks + 1, LINE)),
+            dma((chunks, LINE, n_in - 1)),
+            dma((chunks, LINE, n_in - 1)),
+            dma((chunks, 2, n_grp - 1)),
+            dma((chunks, 2, n_grp - 1)),
+            dma((chunks, n_grp, n_ep)),
+            dma((chunks, n_grp, n_ep)),
+            dma((chunks, n_ep)),
+            dma((chunks, n_ep)),
         ],
         compiler_params=pltpu.CompilerParams(
             collective_id=0, has_side_effects=True, vmem_limit_bytes=67043328),

time: 296 us -> 286 us (0.966)
  Pallas kernels: 286 us -> 275 us
    pallas_call x1, Pallas kernels: 286 us -> 275 us  [run_kernel(): pl.pallas_call(functools.partial(dispatch_kernel, n_ep, n_grp, per_src, t...]
where the time goes in v3:
time: 286 us; the launch traced here: 284 us
  Pallas kernels  275 us (96%)
  local copies, waits for them, and re-layouts  3.97 us (1%)
  blocking collectives  2.93 us (1%)
    pallas_call x1, Pallas kernels, run_kernel(): pl.pallas_call(functools.partial(dispatch_kernel, n_ep, n_grp, per_src, t...  275 us

profile of v3, /device:TPU:12, one launch (start us, length us, event | category | flops | bytes accessed | tf_op | source)
XLA Modules:
  0.0 284.3 jit_solution(16674256477493842657)
XLA Ops:
  0.0 2.9 %all-gather = s32[2,1,16]{2,1,0:T(1,128)} all-gather(s32[1,1,16]{2,1,0:T(1,128)} %bitcast.9), channel_id=1, replica_groups=mesh['grp'=2,'ep'=16] {'grp'}, dimensions={0}, use_global_device_ids=true | all-gather | bytes 192 | tf_op jit(solution)/shard_map/all_gather | solution.py:375
  2.9 0.7 fusion.4
  3.7 1.3 pad_maximum_fusion.meta_hbm
  5.0 275.4 %shard_map.55 = f32[16,48,1024]{2,1,0:T(8,128)} custom-call(s32[2,16]{1,0:T(2,128)} %bitcast.8, f32[16,512]{1,0:T(8,128)} %pad_maximum_fusion.meta_hbm, bf16[512,2048]{1,0:T(8,128)(2,1)} %og_hbm.1, bf16[3072,1536]{1,0:T(8,128)(2,1)} %gu_hbm.1), custom_call_target="tpu_custom_call" | custom-call | tf_op jit(solution)/shard_map/pallas_call | solution.py:328
  280.4 4.0 %copy.7 = f32[1,768,1024]{2,1,0:T(8,128)} copy(f32[1,768,1024]{2,1,0:T(8,128)} %bitcast.6) | data formatting | bytes 6291456
